TPU v7x, 256 devices: a whole 4x4x8 slice. The times are simulated.
256 devices in a mesh: row: 8 (over y, core), col: 32 (over z, x).
Axes of the slice: x: 4, y: 4, z: 8, core: 2. Of those that a mesh axis runs over, the one named last changes fastest.
Arguments:
- ancestor: bfloat16 [16384, 16384], P('row', 'col'), may hold values from -6 to 6, as said below
- panels: bfloat16 [3, 512, 16384], P(None, 'col', 'row'), may hold values from -0.0625 to 0.0625
- diag_inverse: float32 [3, 512, 512], replicated, may hold values from -6 to 6, as said below
- supernode_blocks: int32 [3, 4], replicated, may hold values from 0 to 127, as said below
- row_lists: int32 [3, 64], replicated, may hold values from 0 to 127, as said below
Outputs:
- updated: bfloat16 [16384, 16384], P('row', 'col')
Inputs may be any that keep to these rules, and one draw needn't show every extreme that they name: ancestor is exactly symmetric. `diag_inverse`: each supernode's block is exactly symmetric. `supernode_blocks`: the 3 times 512 / 128 block numbers are all distinct. `row_lists`: each row holds 64 distinct block numbers; row s holds every block of the supernodes before s and none of supernode s or of later ones.
All inputs are finite; a program needn't handle non-finite values.
Results may differ from a plain program's by a relative error of at most 0.002.
Values may be sent and summed in bfloat16 or wider, within the bound.
No kernel may reach another device: no remote copies, remote signals or barrier semaphores. Data moves between devices by JAX's collectives and lax.ppermute only.
A program may use at most 64 MiB of HBM per device.

v0:
```python
import jax
import jax.numpy as jnp
from jax import lax
from jax.sharding import PartitionSpec as P

W = 512
B = 128
S = 3


def spread(value, axis, source):
    kept = jnp.where(lax.axis_index(axis) == source, value, 0).astype(value.dtype)
    return lax.psum(kept, axis)


def block_flags(listed, first_block, block_count):
    block_ids = first_block + jnp.arange(block_count, dtype=jnp.int32)
    return jnp.any(block_ids[:, None] == listed[None, :], axis=1)


def local(ancestor, panels, diag_inverse, supernode_blocks, row_lists):
    row_count = lax.axis_size("row")
    col_count = lax.axis_size("col")
    row_pos = lax.axis_index("row")
    col_pos = lax.axis_index("col")
    local_rows, local_cols = ancestor.shape
    per_node = W // B
    row_blocks = local_rows // B
    col_blocks = local_cols // B
    col_ratio = col_count // row_count
    first_rowblock = row_pos * row_blocks
    first_colblock = col_pos * col_blocks
    current = ancestor
    for supernode in range(S):
        listed = row_lists[supernode]
        owned_blocks = supernode_blocks[supernode]
        row_flags = block_flags(listed, first_rowblock, row_blocks)
        col_flags = block_flags(listed, first_colblock, col_blocks)
        panel_rows = lax.all_gather(panels[supernode], "col", axis=0, tiled=True)
        panel_rows = jnp.where(
            row_flags[None, :, None], panel_rows.reshape(W, row_blocks, B), 0
        ).reshape(W, local_rows)
        partial_value = -lax.dot_general(
            current, panel_rows, (((0,), (1,)), ((), ())), preferred_element_type=jnp.float32
        )
        col_sum = lax.psum(partial_value, "row")
        col_update = (
            jnp.where(col_flags[:, None, None], col_sum.reshape(col_blocks, B, W), 0.0)
            .reshape(local_cols, W)
            .astype(jnp.bfloat16)
        )
        slab_list = [
            spread(col_update, "col", col_ratio * row_pos + shift_idx)
            for shift_idx in range(col_ratio)
        ]
        row_update = jnp.concatenate(slab_list, axis=0)
        cross_part = jnp.dot(panel_rows, row_update, preferred_element_type=jnp.float32)
        cross_term = lax.psum(cross_part.astype(jnp.bfloat16), "row").astype(jnp.float32)
        diag_block = (diag_inverse[supernode] - 0.5 * (cross_term + cross_term.T)).astype(
            jnp.bfloat16
        )
        col_match = (first_colblock + jnp.arange(col_blocks, dtype=jnp.int32))[
            :, None
        ] == owned_blocks[None, :]
        row_match = (first_rowblock + jnp.arange(row_blocks, dtype=jnp.int32))[
            :, None
        ] == owned_blocks[None, :]
        col_hit = jnp.any(col_match, axis=1)
        row_hit = jnp.any(row_match, axis=1)
        col_select = col_match.astype(jnp.bfloat16)
        row_select = row_match.astype(jnp.bfloat16)
        column_fill = jnp.einsum(
            "rkb,jk->rjb",
            row_update.reshape(local_rows, per_node, B),
            col_select,
            preferred_element_type=jnp.float32,
        ).astype(jnp.bfloat16)
        blocks_view = jnp.where(
            col_hit[None, :, None], column_fill, current.reshape(local_rows, col_blocks, B)
        )
        row_fill = jnp.einsum(
            "jkb,ik->ibj",
            col_update.reshape(local_cols, per_node, B),
            row_select,
            preferred_element_type=jnp.float32,
        ).astype(jnp.bfloat16)
        rows_view = jnp.where(
            row_hit[:, None, None], row_fill, blocks_view.reshape(row_blocks, B, local_cols)
        )
        corner = jnp.einsum(
            "ik,kalb,jl->iajb",
            row_select,
            diag_block.reshape(per_node, B, per_node, B),
            col_select,
            preferred_element_type=jnp.float32,
        ).astype(jnp.bfloat16)
        corner_hit = row_hit[:, None, None, None] & col_hit[None, None, :, None]
        grid_view = jnp.where(corner_hit, corner, rows_view.reshape(row_blocks, B, col_blocks, B))
        current = grid_view.reshape(local_rows, local_cols)
    return current


def solution(mesh):
    in_specs = (P("row", "col"), P(None, "col", "row"), P(), P(), P())
    out_specs = P("row", "col")
    return jax.shard_map(local, mesh=mesh, in_specs=in_specs, out_specs=out_specs, check_vma=False)
```

profile of v0, /device:TPU:2, one launch (start us, length us, event | category | flops | bytes accessed | tf_op | source)
XLA Modules:
  0.0 1100.6 jit_solution(17126207968095562700)
XLA Ops:
  9.6 79.9 %all-gather.11.cloned.1.call-done = bf16[1,512,2048]{2,1,0:T(8,128)(2,1)} async-done(((bf16[1,16,2048]{2,1,0:T(8,128)(2,1)}), bf16[1,512,2048]{2,1,0:T(8,128)(2,1)}) %all-gather.11.cloned.1.call-update) | async-done | bytes 2097168 | tf_op jit(solution)/shard_map/all_gather | solution.py:39
  89.5 3.5 fusion.11
  93.0 50.2 %all-reduce.24 = bf16[512,512]{0,1:T(8,128)(2,1)S(1)} all-reduce(f32[512,512]{0,1:T(8,128)S(1)} %fusion.11), channel_id=1, replica_groups=mesh['row'=8,'col'=32] {'row'}, use_global_device_ids=true, to_apply=%region_12.13 | all-reduce | flops 262144 | bytes 1572864 | tf_op jit(solution)/shard_map/psum | solution.py:46
  145.5 152.2 %all-reduce.23.cloned.1.call-done = (bf16[512,512]{0,1:T(8,128)(2,1)}, bf16[512,512]{0,1:T(8,128)(2,1)}, bf16[512,512]{0,1:T(8,128)(2,1)}, bf16[512,512]{0,1:T(8,128)(2,1)}) async-done(((bf16[512,512]{0,1:T(8,128)(2,1)}, bf16[512,512]{0,1:T(8,128)(2,1)}, bf16[512,512]{0,1:T(8,128)(2,1)}, bf16[512,512]{0,1:T(8,128)(2,1)}), (bf16[512,512]{0,1:T(8,128)(2,1)}, bf16[512,512]{0,1:T(8,128)(2,1)}, ...) | async-done | bytes 2097168 | tf_op jit(solution)/shard_map/psum | solution.py:13
  300.2 2.1 fusion.18
  303.0 4.0 reshape.191
  307.8 2.6 copy.55
  310.4 3.8 bitcast_select_fusion.6
  314.2 2.2 reshape.222
  316.4 3.4 copy.95
  319.9 2.3 bitcast_select_fusion.7
  322.2 5.1 copy.58
  327.3 40.0 %all-reduce.13.cloned.1.call-done = bf16[512,512]{1,0:T(8,128)(2,1)} async-done(((bf16[512,512]{1,0:T(8,128)(2,1)}), bf16[512,512]{1,0:T(8,128)(2,1)}) %all-reduce.13.cloned.1.call-update) | async-done | bytes 524304 | tf_op jit(solution)/shard_map/psum | solution.py:58
  368.6 1.7 fusion.29
  370.9 2.6 bitcast_select_fusion.8
  373.5 3.7 copy.59
  377.2 68.5 %all-gather.9.cloned.1.call-done = bf16[1,512,2048]{2,1,0:T(8,128)(2,1)} async-done(((bf16[1,16,2048]{2,1,0:T(8,128)(2,1)}), bf16[1,512,2048]{2,1,0:T(8,128)(2,1)}) %all-gather.9.cloned.1.call-update) | async-done | bytes 2097168 | tf_op jit(solution)/shard_map/all_gather | solution.py:39
  445.7 4.5 fusion.12
  450.2 51.0 %all-reduce.25 = bf16[512,512]{0,1:T(8,128)(2,1)S(1)} all-reduce(f32[512,512]{0,1:T(8,128)} %fusion.12), channel_id=1, replica_groups=mesh['row'=8,'col'=32] {'row'}, use_global_device_ids=true, to_apply=%region_18.19 | all-reduce | flops 262144 | bytes 1572864 | tf_op jit(solution)/shard_map/psum | solution.py:46
  503.4 152.1 %all-reduce.21.cloned.1.call-done = (bf16[512,512]{0,1:T(8,128)(2,1)}, bf16[512,512]{0,1:T(8,128)(2,1)}, bf16[512,512]{0,1:T(8,128)(2,1)}, bf16[512,512]{0,1:T(8,128)(2,1)}) async-done(((bf16[512,512]{0,1:T(8,128)(2,1)}, bf16[512,512]{0,1:T(8,128)(2,1)}, bf16[512,512]{0,1:T(8,128)(2,1)}, bf16[512,512]{0,1:T(8,128)(2,1)}), (bf16[512,512]{0,1:T(8,128)(2,1)}, bf16[512,512]{0,1:T(8,128)(2,1)}, ...) | async-done | bytes 2097168 | tf_op jit(solution)/shard_map/psum | solution.py:13
  659.4 2.1 fusion.19
  662.5 1.9 copy.66
  664.7 4.4 copy.65
  669.1 5.2 bitcast_select_fusion.3
  674.3 4.1 reshape.223
  678.4 3.4 copy.98
  681.9 2.3 bitcast_select_fusion.4
  684.2 5.1 copy.70
  689.3 37.2 %all-reduce.15.cloned.1.call-done = bf16[512,512]{0,1:T(8,128)(2,1)} async-done(((bf16[512,512]{0,1:T(8,128)(2,1)}), bf16[512,512]{0,1:T(8,128)(2,1)}) %all-reduce.15.cloned.1.call-update) | async-done | bytes 524304 | tf_op jit(solution)/shard_map/psum | solution.py:58
  727.8 1.7 fusion.26
  730.1 2.6 bitcast_select_fusion.5
  732.7 3.7 copy.71
  736.4 68.6 %all-gather.7.cloned.1.call-done = bf16[1,512,2048]{2,1,0:T(8,128)(2,1)} async-done(((bf16[1,16,2048]{2,1,0:T(8,128)(2,1)}), bf16[1,512,2048]{2,1,0:T(8,128)(2,1)}) %all-gather.7.cloned.1.call-update) | async-done | bytes 2097168 | tf_op jit(solution)/shard_map/all_gather | solution.py:39
  805.0 4.5 fusion.15
  809.5 50.8 %all-reduce.26 = bf16[512,512]{0,1:T(8,128)(2,1)S(1)} all-reduce(f32[512,512]{0,1:T(8,128)} %fusion.15), channel_id=1, replica_groups=mesh['row'=8,'col'=32] {'row'}, use_global_device_ids=true, to_apply=%region_24.25 | all-reduce | flops 262144 | bytes 1572864 | tf_op jit(solution)/shard_map/psum | solution.py:46
  862.9 1.9 copy.78
  865.1 149.7 %all-reduce.19.cloned.1.call-done = (bf16[512,512]{0,1:T(8,128)(2,1)}, bf16[512,512]{0,1:T(8,128)(2,1)}, bf16[512,512]{0,1:T(8,128)(2,1)}, bf16[512,512]{0,1:T(8,128)(2,1)}) async-done(((bf16[512,512]{0,1:T(8,128)(2,1)}, bf16[512,512]{0,1:T(8,128)(2,1)}, bf16[512,512]{0,1:T(8,128)(2,1)}, bf16[512,512]{0,1:T(8,128)(2,1)}), (bf16[512,512]{0,1:T(8,128)(2,1)}, bf16[512,512]{0,1:T(8,128)(2,1)}, ...) | async-done | bytes 2097168 | tf_op jit(solution)/shard_map/psum | solution.py:13
  1017.3 2.1 fusion.20
  1019.5 2.6 copy.77
  1022.0 4.5 bitcast_select_fusion
  1026.6 2.2 reshape.224
  1028.8 3.4 copy.101
  1032.2 2.3 bitcast_select_fusion.1
  1034.6 4.2 copy.82
  1038.8 45.6 %all-reduce.17.cloned.1.call-done = bf16[512,512]{0,1:T(8,128)(2,1)} async-done(((bf16[512,512]{0,1:T(8,128)(2,1)}), bf16[512,512]{0,1:T(8,128)(2,1)}) %all-reduce.17.cloned.1.call-update) | async-done | bytes 524304 | tf_op jit(solution)/shard_map/psum | solution.py:58
  1085.7 2.4 fusion.23
  1090.8 1.6 copy.104
  1092.4 1.7 copy.130
  (90 shorter events, 29.3 us)
Async XLA Ops:
  6.5 83.0 %all-gather.11.cloned.1.call-start = ((), (), s32[]{:S(2)}) async-start(), calls=%async_computation.5 | async-start | bytes 2162688 | tf_op jit(solution)/shard_map/all_gather | solution.py:39
  8.1 289.5 %all-reduce.23.cloned.1.call-start = ((), (), s32[]{:S(2)}) async-start(), calls=%async_computation.8 | async-start | bytes 4194304 | tf_op jit(solution)/shard_map/psum | solution.py:13
  145.4 222.0 %all-reduce.13.cloned.1.call-start = ((), (), s32[]{:S(2)}) async-start(), calls=%async_computation | async-start | bytes 1048576 | tf_op jit(solution)/shard_map/psum | solution.py:58
  297.6 2.4 copy-start.6
  297.6 2.5 copy-start.4
  297.6 2.5 copy-start.9
  302.3 143.4 %all-gather.9.cloned.1.call-start = ((), (), s32[]{:S(2)}) async-start(), calls=%async_computation.4 | async-start | bytes 2162688 | tf_op jit(solution)/shard_map/all_gather | solution.py:39
  302.9 4.0 copy-start.8
  302.9 352.6 %all-reduce.21.cloned.1.call-start = ((), (), s32[]{:S(2)}) async-start(), calls=%async_computation.7 | async-start | bytes 4194304 | tf_op jit(solution)/shard_map/psum | solution.py:13
  503.4 223.2 %all-reduce.15.cloned.1.call-start = ((), (), s32[]{:S(2)}) async-start(), calls=%async_computation.1 | async-start | bytes 1048576 | tf_op jit(solution)/shard_map/psum | solution.py:58
  655.6 2.4 copy-start.7
  655.6 2.4 copy-start.5
  655.6 3.8 copy-start.10
  658.1 1.3 copy-start
  661.5 143.5 %all-gather.7.cloned.1.call-start = ((), (), s32[]{:S(2)}) async-start(), calls=%async_computation.3 | async-start | bytes 2162688 | tf_op jit(solution)/shard_map/all_gather | solution.py:39
  662.3 352.5 %all-reduce.19.cloned.1.call-start = ((), (), s32[]{:S(2)}) async-start(), calls=%async_computation.6 | async-start | bytes 4194304 | tf_op jit(solution)/shard_map/psum | solution.py:13
  664.7 4.4 copy-start.1
  862.6 221.9 %all-reduce.17.cloned.1.call-start = ((), (), s32[]{:S(2)}) async-start(), calls=%async_computation.2 | async-start | bytes 1048576 | tf_op jit(solution)/shard_map/psum | solution.py:58
  1014.8 2.4 copy-start.3
  1014.8 2.5 copy-start.2
  1014.8 2.5 copy-start.11
Sparse Core Ops, SparseCore 0:
  9.9 79.5 all-gather.10
  145.5 152.0 all-reduce.22
  302.4 64.8 all-reduce.12
  369.8 75.8 all-gather.8
  503.5 152.0 all-reduce.20
  661.6 64.8 all-reduce.14
  729.2 75.8 all-gather.6
  862.7 152.0 all-reduce.18
  1019.6 64.8 all-reduce.16
where the time goes:
time: 1100 us
  waiting for transfers between devices  795 us (72%)
  blocking collectives  152 us (14%)
  local copies, waits for them, and re-layouts  79 us (7%)
  matrix products  47 us (4%)
  between operations  13.6 us (1%)
  other arithmetic  13.1 us (1%)
    psum x3, waiting for transfers between devices, spread(): return lax.psum(kept, axis)  454 us
    all_gather x3, waiting for transfers between devices, local(): panel_rows = lax.all_gather(panels[supernode], 'col', axis=0, tiled=True)  217 us
    psum x3, blocking collectives, local(): col_sum = lax.psum(partial_value, 'row')  152 us
    psum x3, waiting for transfers between devices, local(): lax.psum(cross_part.astype(jnp.bfloat16), 'row').astype(jnp.float32)  123 us
  transfers between devices with their start and end apart: 9, of which 9 were waited for; matrix products, arithmetic and copies ran while one was open for 9% of the time, Pallas kernels for 0%

commit v1 on v0

--- a/solution.py
+++ b/solution.py
@@ -36,7 +36,10 @@
         owned_blocks = supernode_blocks[supernode]
         row_flags = block_flags(listed, first_rowblock, row_blocks)
         col_flags = block_flags(listed, first_colblock, col_blocks)
-        panel_rows = lax.all_gather(panels[supernode], "col", axis=0, tiled=True)
+        panel_rows = jnp.concatenate(
+            lax.all_to_all(jnp.stack([panels[supernode]] * lax.axis_size("col")), "col", 0, 0),
+            axis=0,
+        )
         panel_rows = jnp.where(
             row_flags[None, :, None], panel_rows.reshape(W, row_blocks, B), 0
         ).reshape(W, local_rows)

time: 1100 us -> 995 us (0.905)
  waiting for transfers between devices: 795 us -> 639 us
  starting transfers between devices: 0.55 us -> 29.8 us
  other arithmetic: 13.1 us -> 25.7 us
    all_gather x3 -> x0, waiting for transfers between devices: 217 us -> none  [local(): panel_rows = lax.all_gather(panels[supernode], 'col', axis=0, tiled=True)]
    all_to_all x0 -> x3, waiting for transfers between devices: none -> 48.6 us  [local(): lax.all_to_all(jnp.stack([panels[supernode]] * lax.axis_size('col')), 'co...]
    all_to_all x0 -> x3, starting transfers between devices: none -> 28.7 us  [local(): lax.all_to_all(jnp.stack([panels[supernode]] * lax.axis_size('col')), 'co...]
    select_n x0 -> x5, other arithmetic: none -> 12.5 us  [local(): jnp.where(row_flags[None, :, None], panel_rows.reshape(W, row_blocks, B), 0)]
    psum x3, waiting for transfers between devices: 123 us -> 135 us  [local(): lax.psum(cross_part.astype(jnp.bfloat16), 'row').astype(jnp.float32)]
  transfers between devices with their start and end apart: 9 -> 9, of which waited for: 9 -> 7; matrix products, arithmetic and copies ran while one was open for 9% -> 11% of each run, Pallas kernels for 0% -> 0%
where the time goes in v1:
time: 995 us; the launch traced here: 989 us
  waiting for transfers between devices  639 us (64%)
  blocking collectives  156 us (16%)
  local copies, waits for them, and re-layouts  79.2 us (8%)
  matrix products  45.2 us (5%)
  starting transfers between devices  29.8 us (3%)
  other arithmetic  25.7 us (3%)
  between operations  14.2 us (1%)
    psum x3, waiting for transfers between devices, spread(): return lax.psum(kept, axis)  455 us
    psum x3, blocking collectives, local(): col_sum = lax.psum(partial_value, 'row')  156 us
    psum x3, waiting for transfers between devices, local(): lax.psum(cross_part.astype(jnp.bfloat16), 'row').astype(jnp.float32)  135 us
    all_to_all x3, waiting for transfers between devices, local(): lax.all_to_all(jnp.stack([panels[supernode]] * lax.axis_size('col')), 'co...  48.6 us
    all_to_all x3, starting transfers between devices, local(): lax.all_to_all(jnp.stack([panels[supernode]] * lax.axis_size('col')), 'co...  28.7 us
  transfers between devices with their start and end apart: 9, of which 7 were waited for; matrix products, arithmetic and copies ran while one was open for 11% of the time, Pallas kernels for 0%

profile of v1, /device:TPU:2, one launch (start us, length us, event | category | flops | bytes accessed | tf_op | source)
XLA Modules:
  0.0 989.4 jit_solution(12574699022169464330)
XLA Ops:
  9.0 11.7 %all-to-all-start.2 = ((bf16[32,16,2048]{2,1,0:T(8,128)(2,1)}), bf16[32,16,2048]{2,1,0:T(8,128)(2,1)S(1)}, u32[]{:S(2)}, u32[]{:S(2)}) async-start(bf16[32,16,2048]{2,1,0:T(8,128)(2,1)} %stack.11), calls=%async_computation.2 | async-start | bytes 4194304 | tf_op jit(solution)/shard_map/all_to_all | solution.py:40
  21.4 48.6 %all-to-all-done.2 = bf16[32,16,2048]{2,1,0:T(8,128)(2,1)S(1)} async-done(((bf16[32,16,2048]{2,1,0:T(8,128)(2,1)}), bf16[32,16,2048]{2,1,0:T(8,128)(2,1)S(1)}, u32[]{:S(2)}, u32[]{:S(2)}) %all-to-all-start.2) | async-done | bytes 2097184 | tf_op jit(solution)/shard_map/all_to_all | solution.py:40
  72.0 6.9 all-to-all-start.1
  79.0 1.9 bitcast_select_fusion.9
  82.2 2.2 fusion.12
  84.4 52.9 %all-reduce.24 = bf16[512,512]{0,1:T(8,128)(2,1)S(1)} all-reduce(f32[512,512]{0,1:T(8,128)} %fusion.12), channel_id=1, replica_groups=mesh['row'=8,'col'=32] {'row'}, use_global_device_ids=true, to_apply=%region_12.13 | all-reduce | flops 262144 | bytes 1572864 | tf_op jit(solution)/shard_map/psum | solution.py:49
  139.6 4.0 reshape.206
  146.2 10.1 %all-to-all-start = ((bf16[32,16,2048]{2,1,0:T(8,128)(2,1)}), bf16[32,16,2048]{2,1,0:T(8,128)(2,1)}, u32[]{:S(2)}, u32[]{:S(2)}) async-start(bf16[32,16,2048]{2,1,0:T(8,128)(2,1)} %stack.9), calls=%async_computation | async-start | bytes 4194304 | tf_op jit(solution)/shard_map/all_to_all | solution.py:40
  157.9 160.8 %all-reduce.23.cloned.1.call-done = (bf16[512,512]{0,1:T(8,128)(2,1)}, bf16[512,512]{0,1:T(8,128)(2,1)}, bf16[512,512]{0,1:T(8,128)(2,1)}, bf16[512,512]{0,1:T(8,128)(2,1)}) async-done(((bf16[512,512]{0,1:T(8,128)(2,1)}, bf16[512,512]{0,1:T(8,128)(2,1)}, bf16[512,512]{0,1:T(8,128)(2,1)}, bf16[512,512]{0,1:T(8,128)(2,1)}), (bf16[512,512]{0,1:T(8,128)(2,1)}, bf16[512,512]{0,1:T(8,128)(2,1)}, ...) | async-done | bytes 2097168 | tf_op jit(solution)/shard_map/psum | solution.py:13
  321.3 2.1 convolution_convert_fusion.2
  323.9 2.6 copy.55
  326.5 3.8 bitcast_select_fusion.6
  330.3 2.2 reshape.234
  332.5 3.4 copy.95
  336.0 2.3 bitcast_select_fusion.7
  338.3 5.1 copy.58
  343.4 45.0 %all-reduce.13.cloned.1.call-done = bf16[512,512]{1,0:T(8,128)(2,1)} async-done(((bf16[512,512]{1,0:T(8,128)(2,1)}), bf16[512,512]{1,0:T(8,128)(2,1)}) %all-reduce.13.cloned.1.call-update) | async-done | bytes 524304 | tf_op jit(solution)/shard_map/psum | solution.py:61
  392.0 2.6 bitcast_select_fusion.8
  394.6 3.7 copy.59
  398.3 4.5 fusion.6
  402.8 51.7 %all-reduce.25 = bf16[512,512]{0,1:T(8,128)(2,1)S(1)} all-reduce(f32[512,512]{0,1:T(8,128)} %fusion.6), channel_id=1, replica_groups=mesh['row'=8,'col'=32] {'row'}, use_global_device_ids=true, to_apply=%region_18.19 | all-reduce | flops 262144 | bytes 1572864 | tf_op jit(solution)/shard_map/psum | solution.py:49
  456.9 3.1 bitcast_select_fusion.10
  459.9 3.0 broadcast_select_fusion
  463.0 1.9 copy.66
  465.1 145.7 %all-reduce.21.cloned.1.call-done = (bf16[512,512]{0,1:T(8,128)(2,1)}, bf16[512,512]{0,1:T(8,128)(2,1)}, bf16[512,512]{0,1:T(8,128)(2,1)}, bf16[512,512]{0,1:T(8,128)(2,1)}) async-done(((bf16[512,512]{0,1:T(8,128)(2,1)}, bf16[512,512]{0,1:T(8,128)(2,1)}, bf16[512,512]{0,1:T(8,128)(2,1)}, bf16[512,512]{0,1:T(8,128)(2,1)}), (bf16[512,512]{0,1:T(8,128)(2,1)}, bf16[512,512]{0,1:T(8,128)(2,1)}, ...) | async-done | bytes 2097168 | tf_op jit(solution)/shard_map/psum | solution.py:13
  613.4 2.2 convolution_convert_fusion.1
  615.8 2.6 copy.65
  618.4 4.5 bitcast_select_fusion.3
  623.0 2.2 reshape.235
  625.2 3.4 copy.98
  628.6 2.3 bitcast_select_fusion.4
  631.0 5.1 copy.70
  636.1 44.5 %all-reduce.15.cloned.1.call-done = bf16[512,512]{0,1:T(8,128)(2,1)} async-done(((bf16[512,512]{0,1:T(8,128)(2,1)}), bf16[512,512]{0,1:T(8,128)(2,1)}) %all-reduce.15.cloned.1.call-update) | async-done | bytes 524304 | tf_op jit(solution)/shard_map/psum | solution.py:61
  684.1 2.6 bitcast_select_fusion.5
  686.7 3.7 copy.71
  690.4 4.5 fusion.9
  694.9 51.7 %all-reduce.26 = bf16[512,512]{0,1:T(8,128)(2,1)S(1)} all-reduce(f32[512,512]{0,1:T(8,128)} %fusion.9), channel_id=1, replica_groups=mesh['row'=8,'col'=32] {'row'}, use_global_device_ids=true, to_apply=%region_24.25 | all-reduce | flops 262144 | bytes 1572864 | tf_op jit(solution)/shard_map/psum | solution.py:49
  749.1 3.0 bitcast_select_fusion.11
  754.3 148.6 %all-reduce.19.cloned.1.call-done = (bf16[512,512]{0,1:T(8,128)(2,1)}, bf16[512,512]{0,1:T(8,128)(2,1)}, bf16[512,512]{0,1:T(8,128)(2,1)}, bf16[512,512]{0,1:T(8,128)(2,1)}) async-done(((bf16[512,512]{0,1:T(8,128)(2,1)}, bf16[512,512]{0,1:T(8,128)(2,1)}, bf16[512,512]{0,1:T(8,128)(2,1)}, bf16[512,512]{0,1:T(8,128)(2,1)}), (bf16[512,512]{0,1:T(8,128)(2,1)}, bf16[512,512]{0,1:T(8,128)(2,1)}, ...) | async-done | bytes 2097168 | tf_op jit(solution)/shard_map/psum | solution.py:13
  905.5 2.2 convolution_convert_fusion
  907.7 2.6 copy.77
  910.2 4.5 bitcast_select_fusion
  914.8 2.2 reshape.236
  917.0 3.4 copy.101
  920.4 2.3 bitcast_select_fusion.1
  922.8 4.2 copy.82
  927.0 45.6 %all-reduce.17.cloned.1.call-done = bf16[512,512]{0,1:T(8,128)(2,1)} async-done(((bf16[512,512]{0,1:T(8,128)(2,1)}), bf16[512,512]{0,1:T(8,128)(2,1)}) %all-reduce.17.cloned.1.call-update) | async-done | bytes 524304 | tf_op jit(solution)/shard_map/psum | solution.py:61
  973.9 2.4 fusion.15
  (101 shorter events, 42.7 us)
Async XLA Ops:
  9.0 11.8 %copy-start.13 = (s32[3,64]{1,0:T(4,128)S(1)}, s32[3,64]{1,0:T(4,128)}, u32[]{:S(2)}) copy-start(s32[3,64]{1,0:T(4,128)} %param.9) | copy-start | bytes 2308
  9.0 61.0 %all-to-all-start.2 = ((bf16[32,16,2048]{2,1,0:T(8,128)(2,1)}), bf16[32,16,2048]{2,1,0:T(8,128)(2,1)S(1)}, u32[]{:S(2)}, u32[]{:S(2)}) async-start(bf16[32,16,2048]{2,1,0:T(8,128)(2,1)} %stack.11), calls=%async_computation.2 | async-start | bytes 4194304 | tf_op jit(solution)/shard_map/all_to_all | solution.py:40
  70.0 2.0 copy-start.1
  72.0 72.4 %all-to-all-start.1 = ((bf16[32,16,2048]{2,1,0:T(8,128)(2,1)}), bf16[32,16,2048]{2,1,0:T(8,128)(2,1)S(1)}, u32[]{:S(2)}, u32[]{:S(2)}) async-start(bf16[32,16,2048]{2,1,0:T(8,128)(2,1)} %stack.10), calls=%async_computation.1 | async-start | bytes 4194304 | tf_op jit(solution)/shard_map/all_to_all | solution.py:40
  78.9 239.8 %all-reduce.23.cloned.1.call-start = ((), (), s32[]{:S(2)}) async-start(), calls=%async_computation.8 | async-start | bytes 4194304 | tf_op jit(solution)/shard_map/psum | solution.py:13
  78.9 3.2 copy-start.2
  80.8 1.3 copy-start.3
  139.6 4.0 copy-start.14
  144.4 12.0 %copy-start = (bf16[32,16,2048]{2,1,0:T(8,128)(2,1)}, bf16[32,16,2048]{2,1,0:T(8,128)(2,1)S(1)}, u32[]{:S(2)}) copy-start(bf16[32,16,2048]{2,1,0:T(8,128)(2,1)S(1)} %all-to-all-done.1) | copy-start | bytes 6291460
  146.2 313.7 %all-to-all-start = ((bf16[32,16,2048]{2,1,0:T(8,128)(2,1)}), bf16[32,16,2048]{2,1,0:T(8,128)(2,1)}, u32[]{:S(2)}, u32[]{:S(2)}) async-start(bf16[32,16,2048]{2,1,0:T(8,128)(2,1)} %stack.9), calls=%async_computation | async-start | bytes 4194304 | tf_op jit(solution)/shard_map/all_to_all | solution.py:40
  156.3 232.1 %all-reduce.13.cloned.1.call-start = ((), (), s32[]{:S(2)}) async-start(), calls=%async_computation.3 | async-start | bytes 1048576 | tf_op jit(solution)/shard_map/psum | solution.py:61
  318.7 2.4 copy-start.8
  318.7 2.5 copy-start.7
  318.7 2.5 copy-start.4
  323.4 287.4 %all-reduce.21.cloned.1.call-start = ((), (), s32[]{:S(2)}) async-start(), calls=%async_computation.7 | async-start | bytes 4194304 | tf_op jit(solution)/shard_map/psum | solution.py:13
  456.7 223.9 %all-reduce.15.cloned.1.call-start = ((), (), s32[]{:S(2)}) async-start(), calls=%async_computation.4 | async-start | bytes 1048576 | tf_op jit(solution)/shard_map/psum | solution.py:61
  610.8 2.4 copy-start.10
  610.8 2.5 copy-start.9
  610.8 2.5 copy-start.5
  615.6 287.3 %all-reduce.19.cloned.1.call-start = ((), (), s32[]{:S(2)}) async-start(), calls=%async_computation.6 | async-start | bytes 4194304 | tf_op jit(solution)/shard_map/psum | solution.py:13
  748.7 223.9 %all-reduce.17.cloned.1.call-start = ((), (), s32[]{:S(2)}) async-start(), calls=%async_computation.5 | async-start | bytes 1048576 | tf_op jit(solution)/shard_map/psum | solution.py:61
  902.9 2.4 copy-start.12
  902.9 2.5 copy-start.11
  902.9 2.5 copy-start.6
Sparse Core Ops, SparseCore 0:
  139.7 178.9 all-reduce.22
  323.5 64.8 all-reduce.12
  456.8 154.0 all-reduce.20
  615.7 64.8 all-reduce.14
  748.9 154.0 all-reduce.18
  907.8 64.7 all-reduce.16
